TPU v7x, 128 devices: a whole 4x4x4 slice. The times are simulated.
128 devices in a mesh: req: 32 (over y, x, core), mlp: 4 (over z).
Axes of the slice: x: 4, y: 4, z: 4, core: 2. Of those that a mesh axis runs over, the one named last changes fastest.
Arguments:
- states: bfloat16 [8192, 2560], P('req')
- attn_gain: float32 [2560], replicated, may hold values from 0.1 to 1.9
- query_matrix: bfloat16 [2560, 2048], P(None, 'mlp')
- key_matrix: bfloat16 [2560, 1024], P(None, 'mlp')
- value_matrix: bfloat16 [2560, 1024], P(None, 'mlp'), may hold values from -0.125 to 0.125
- query_gain: float32 [256], replicated
- key_gain: float32 [256], replicated
- out_weight: bfloat16 [2048, 2560], P('mlp'), may hold values from -0.125 to 0.125
- post_gain: float32 [2560], replicated, may hold values from 0.1 to 1.9
- ffw_gain: float32 [2560], replicated, may hold values from 0.1 to 1.9
- gate_weight: bfloat16 [2560, 10240], P(None, 'req'), may hold values from -0.125 to 0.125
- up_weight: bfloat16 [2560, 10240], P(None, 'req'), may hold values from -0.125 to 0.125
- down_weight: bfloat16 [10240, 2560], P('req'), may hold values from -0.0625 to 0.0625
- post_ffw_gain: float32 [2560], replicated, may hold values from 0.1 to 1.9
- prefix_key_cache: bfloat16 [32, 512, 1024], P('req', None, 'mlp')
- prefix_value_cache: bfloat16 [32, 512, 1024], P('req', None, 'mlp'), may hold values from -6 to 6
- segment: int32 [8192], P('req'), may hold values from 0 to 15, as said below
- prefix_id: int32 [8192], P('req'), may hold values from 0 to 31, as said below
- owner_map: int32 [32], replicated, may hold values from 0 to 31, each once
Outputs:
- layer_out: bfloat16 [8192, 2560], P(('req', 'mlp'))
Inputs may be any that keep to these rules, and one draw needn't show every extreme that they name: Within each block of 256 rows, equal segment values mark one request and occupy contiguous rows; requests hold 16 or 32 tokens. `prefix_id`: all tokens of one request name the same prefix group. In each block of 256 rows at most 32 rows name prefix groups of the same owner, and one prefix group is named by exactly 32 rows of every block.
All inputs are finite; a program needn't handle non-finite values.
Results may differ from a plain program's by a relative error of at most 0.017.
The roundings to bfloat16 on the way count: a program that leaves them out, or rounds other values in their place, can miss the bound.
Values may be sent and summed in bfloat16 or wider, within the bound.
A program may use at most 128 MiB of HBM per device.

v0:
```python
import jax
import jax.numpy as jnp
from jax import lax
from jax.sharding import PartitionSpec as P

CAP = 32


EPS = 1e-06


def normed(values_in, gain_vec):
    return (
        values_in
        * lax.rsqrt(jnp.mean(values_in * values_in, axis=-1, keepdims=True) + EPS)
        * gain_vec
    )


def local_attention(query_rows, key_rows, value_rows, segment_rows, score_scale):
    scores = (
        jnp.einsum("tgqd,sgd->gqts", query_rows, key_rows, preferred_element_type=jnp.float32)
        * score_scale
    )
    row_count = segment_rows.shape[0]
    token_position = jnp.arange(row_count, dtype=jnp.int32)
    allowed = (segment_rows[:, None] == segment_rows[None, :]) & (
        token_position[:, None] >= token_position[None, :]
    )
    scores = jnp.where(allowed, scores, -jnp.inf)
    row_max = jnp.max(scores, axis=-1, keepdims=True)
    powers = jnp.exp(scores - row_max)
    row_sum = jnp.sum(powers, axis=-1, keepdims=True)
    weights = (powers / row_sum).astype(jnp.bfloat16)
    mixed = jnp.einsum("gqts,sgd->tgqd", weights, value_rows, preferred_element_type=jnp.float32)
    log_total = jnp.transpose((row_max + jnp.log(row_sum))[..., 0], (2, 0, 1))
    return (mixed, log_total)


def prefix_partials(incoming, stored_keys, stored_values, score_scale):
    sources, slot_count, head_cols = incoming.shape
    kv_heads = stored_keys.shape[1]
    head_dim = stored_keys.shape[2]
    query_group_width = head_cols // (kv_heads * head_dim)
    query_rows = incoming.reshape(sources * slot_count, kv_heads, query_group_width, head_dim)
    scores = (
        jnp.einsum("rgqd,kgd->rgqk", query_rows, stored_keys, preferred_element_type=jnp.float32)
        * score_scale
    )
    row_max = jnp.max(scores, axis=-1, keepdims=True)
    powers = jnp.exp(scores - row_max)
    row_sum = jnp.sum(powers, axis=-1, keepdims=True)
    weights = (powers / row_sum).astype(jnp.bfloat16)
    mixed = jnp.einsum("rgqk,kgd->rgqd", weights, stored_values, preferred_element_type=jnp.float32)
    mixed = lax.optimization_barrier(mixed.astype(jnp.bfloat16)).astype(jnp.float32)
    log_total = row_max[..., 0] + jnp.log(row_sum[..., 0])
    return (
        mixed.reshape(sources, slot_count, head_cols),
        log_total.reshape(sources, slot_count, kv_heads * query_group_width),
    )


def body(
    states,
    attn_gain,
    query_matrix,
    key_matrix,
    value_matrix,
    query_gain,
    key_gain,
    out_weight,
    post_gain,
    ffw_gain,
    gate_weight,
    up_weight,
    down_weight,
    post_ffw_gain,
    prefix_key_cache,
    prefix_value_cache,
    segment,
    prefix_id,
    owner_map,
):
    row_count = states.shape[0]
    head_dim = query_gain.shape[0]
    kv_heads = key_matrix.shape[1] // head_dim
    head_cols = query_matrix.shape[1]
    query_group_width = head_cols // (kv_heads * head_dim)
    score_scale = head_dim ** (-0.5)
    req_count = lax.axis_size("req")
    mlp_count = lax.axis_size("mlp")
    mlp_index = lax.axis_index("mlp")
    quarter = row_count // mlp_count
    states_f = states.astype(jnp.float32)
    normalized_input = normed(states_f, attn_gain).astype(jnp.bfloat16)
    unnormed_queries = jnp.dot(
        normalized_input, query_matrix, preferred_element_type=jnp.float32
    ).reshape(row_count, kv_heads, query_group_width, head_dim)
    query_vectors = normed(unnormed_queries, query_gain).astype(jnp.bfloat16)
    unnormed_keys = jnp.dot(
        normalized_input, key_matrix, preferred_element_type=jnp.float32
    ).reshape(row_count, kv_heads, head_dim)
    key_vectors = normed(unnormed_keys, key_gain).astype(jnp.bfloat16)
    value_vectors = (
        jnp.dot(normalized_input, value_matrix, preferred_element_type=jnp.float32)
        .astype(jnp.bfloat16)
        .reshape(row_count, kv_heads, head_dim)
    )
    prefix_count = owner_map.shape[0]
    prefix_onehot = (
        prefix_id[:, None] == jnp.arange(prefix_count, dtype=jnp.int32)[None, :]
    ).astype(jnp.int32)
    target = jnp.sum(prefix_onehot * owner_map[None, :], axis=1)
    to_owner = (target[:, None] == jnp.arange(req_count, dtype=jnp.int32)[None, :]).astype(
        jnp.float32
    )
    token_position = jnp.arange(row_count, dtype=jnp.int32)
    earlier = (token_position[:, None] > token_position[None, :]).astype(jnp.float32)
    counts = jnp.dot(earlier, to_owner, precision=lax.Precision.HIGHEST)
    slot_index = jnp.sum(to_owner * counts, axis=1).astype(jnp.int32)
    place_row = target * CAP + slot_index
    placing = (place_row[None, :] == jnp.arange(req_count * CAP, dtype=jnp.int32)[:, None]).astype(
        jnp.bfloat16
    )
    outgoing = (
        jnp.dot(
            placing, query_vectors.reshape(row_count, head_cols), preferred_element_type=jnp.float32
        )
        .astype(jnp.bfloat16)
        .reshape(req_count, CAP, head_cols)
    )
    stored_keys = prefix_key_cache[0].reshape(-1, kv_heads, head_dim)
    stored_values = prefix_value_cache[0].reshape(-1, kv_heads, head_dim)
    suffix_output, suffix_log_sum = local_attention(
        query_vectors, key_vectors, value_vectors, segment, score_scale
    )
    mixed, log_total = prefix_partials(
        lax.all_to_all(outgoing, "req", split_axis=0, concat_axis=0, tiled=True),
        stored_keys,
        stored_values,
        score_scale,
    )
    back_out = lax.all_to_all(
        mixed.astype(jnp.bfloat16), "req", split_axis=0, concat_axis=0, tiled=True
    ).astype(mixed.dtype)
    back_lse = lax.all_to_all(
        log_total.astype(jnp.bfloat16), "req", split_axis=0, concat_axis=0, tiled=True
    ).astype(log_total.dtype)
    prefix_out = back_out.reshape(req_count * CAP, head_cols)[place_row].reshape(
        row_count, kv_heads, query_group_width, head_dim
    )
    prefix_lse = back_lse.reshape(req_count * CAP, kv_heads * query_group_width)[place_row].reshape(
        row_count, kv_heads, query_group_width
    )
    prefix_out, prefix_lse = (prefix_out, prefix_lse)
    blend = jax.nn.sigmoid(prefix_lse - suffix_log_sum)[..., None]
    attended = (
        (blend * prefix_out + (1.0 - blend) * suffix_output)
        .astype(jnp.bfloat16)
        .reshape(row_count, head_cols)
    )
    partial_value = jnp.dot(attended, out_weight, preferred_element_type=jnp.float32)
    full_sum = lax.psum(partial_value.astype(jnp.bfloat16), "mlp").astype(jnp.float32)
    summed = lax.dynamic_slice_in_dim(full_sum, mlp_index * quarter, quarter, 0)
    own_rows = lax.dynamic_slice_in_dim(states_f, mlp_index * quarter, quarter, 0)
    residual = own_rows + normed(summed, post_gain)
    ffw_in = normed(residual, ffw_gain).astype(jnp.bfloat16)
    piece = lax.all_gather(ffw_in, "req", axis=0, tiled=True)
    gate_proj = jnp.dot(piece, gate_weight, preferred_element_type=jnp.float32)
    up_proj = jnp.dot(piece, up_weight, preferred_element_type=jnp.float32)
    hidden = (jax.nn.gelu(gate_proj, approximate=True) * up_proj).astype(jnp.bfloat16)
    down_sum = lax.psum_scatter(
        jnp.dot(hidden, down_weight, preferred_element_type=jnp.float32).astype(jnp.bfloat16),
        "req",
        scatter_dimension=0,
        tiled=True,
    ).astype(jnp.float32)
    return (residual + normed(down_sum, post_ffw_gain)).astype(jnp.bfloat16)


def solution(mesh):
    return jax.shard_map(
        body,
        mesh=mesh,
        in_specs=(
            P("req", None),
            P(),
            P(None, "mlp"),
            P(None, "mlp"),
            P(None, "mlp"),
            P(),
            P(),
            P("mlp", None),
            P(),
            P(),
            P(None, "req"),
            P(None, "req"),
            P("req", None),
            P(),
            P("req", None, "mlp"),
            P("req", None, "mlp"),
            P("req"),
            P("req"),
            P(),
        ),
        out_specs=P(("req", "mlp"), None),
        check_vma=False,
    )
```

profile of v0, /device:TPU:0, one launch (start us, length us, event | category | flops | bytes accessed | tf_op | source)
XLA Modules:
  0.0 342.0 jit_solution(14212697419758735946)
XLA Ops:
  6.5 0.0 copy-start
  6.5 0.9 select_reduce_fusion
  7.5 0.2 fusion.29
  7.7 1.7 multiply_reduce_fusion
  9.4 0.7 broadcast_bitcast_fusion
  10.0 4.0 %fusion.66 = (f32[256,512]{1,0:T(8,128)}, f32[256,512]{1,0:T(8,128)}) fusion(bf16[2560,512]{1,0:T(8,128)(2,1)} %param.21, f32[2560]{0:T(1024)} %param.20, f32[256]{0:T(256)S(1)} %add_rsqrt_fusion.2, bf16[256,2560]{1,0:T(8,128)(2,1)} %param.19), kind=kOutput, calls=%fused_computation.108 | convolution fusion | flops 673841152 | bytes 4992000 | tf_op jit(solution)/shard_map/dot_general | solution.py:96
  14.1 1.4 mul.266
  15.5 0.3 reduce_sum.93
  15.8 0.3 mul.267
  16.2 0.0 copy-start.7
  16.2 0.0 copy-start.9
  16.3 1.2 multiply_convert_fusion.2
  17.4 1.5 convolution_convert_fusion.2
  18.9 7.6 %all-to-all-start = ((bf16[32,32,512]{2,1,0:T(8,128)(2,1)}), bf16[32,32,512]{2,1,0:T(8,128)(2,1)}, u32[]{:S(2)}, u32[]{:S(2)}) async-start(bf16[32,32,512]{2,1,0:T(8,128)(2,1)} %bitcast.130), calls=%async_computation | async-start | bytes 2097152 | tf_op jit(solution)/shard_map/all_to_all | solution.py:138
  26.5 0.1 fusion.47
  26.6 0.0 copy-start.3
  26.6 3.2 multiply_reduce_fusion.2
  29.9 13.8 %all-to-all-done = bf16[32,32,512]{2,1,0:T(8,128)(2,1)} async-done(((bf16[32,32,512]{2,1,0:T(8,128)(2,1)}), bf16[32,32,512]{2,1,0:T(8,128)(2,1)}, u32[]{:S(2)}, u32[]{:S(2)}) %all-to-all-start) | async-done | bytes 1048608 | tf_op jit(solution)/shard_map/all_to_all | solution.py:138
  43.7 2.2 reshape.279
  45.9 2.0 bitcast_reduce_fusion
  47.9 0.0 copy-start.1
  47.9 0.0 copy-start.8
  47.9 1.9 copy-done.1
  49.8 0.7 fusion.1
  50.5 0.1 convert_element_type.106
  50.6 0.6 copy.99
  51.2 3.8 %all-to-all-start.1 = ((bf16[32,32,2]{1,2,0:T(2,128)(2,1)}), bf16[32,32,2]{1,2,0:T(2,128)(2,1)S(1)}, u32[]{:S(2)}, u32[]{:S(2)}) async-start(bf16[32,32,2]{1,2,0:T(2,128)(2,1)} %copy.99), calls=%async_computation.1 | async-start | bytes 32768 | tf_op jit(solution)/shard_map/all_to_all | solution.py:146
  55.0 0.0 copy-done.8
  55.0 3.5 %fusion.16 = bf16[1024,1,2,256]{3,0,2,1:T(8,128)(2,1)S(1)} fusion(f32[1024,2]{0,1:T(2,128)S(1)} %fusion.1, f32[1024,2]{0,1:T(2,128)S(1)} %get-tuple-element.9, f32[1024,2,512]{0,2,1:T(8,128)} %copy-done.1, bf16[1,512,256]{2,1,0:T(8,128)(2,1)S(1)} %copy-done.8), kind=kOutput, calls=%fused_computation.26 | convolution fusion | flops 541589504 | bytes 5521408 | tf_op jit(solution)/shard_map/rgqk,kgd->rgqd/dot_general | solution.py:54
  58.5 2.1 copy.106
  60.6 2.6 convert_element_type.114
  63.2 0.0 all-to-all-done.1
  63.2 7.5 %all-to-all-start.2 = ((bf16[32,32,512]{2,1,0:T(8,128)(2,1)}), bf16[32,32,512]{2,1,0:T(8,128)(2,1)}, u32[]{:S(2)}, u32[]{:S(2)}) async-start(bf16[32,32,512]{2,1,0:T(8,128)(2,1)} %convert_element_type.114), calls=%async_computation.2 | async-start | bytes 2097152 | tf_op jit(solution)/shard_map/all_to_all | solution.py:143
  70.7 0.2 all-reduce.2.cloned.1.call-start
  70.9 0.4 fusion.67
  71.3 0.0 copy-start.2
  71.3 0.1 fusion.40
  71.4 0.7 copy-done.2
  72.1 0.3 copy.114
  72.4 0.7 gather_fusion
  73.1 0.1 copy.102
  73.2 14.6 %all-to-all-done.2 = bf16[32,32,512]{2,1,0:T(8,128)(2,1)} async-done(((bf16[32,32,512]{2,1,0:T(8,128)(2,1)}), bf16[32,32,512]{2,1,0:T(8,128)(2,1)}, u32[]{:S(2)}, u32[]{:S(2)}) %all-to-all-start.2) | async-done | bytes 1048608 | tf_op jit(solution)/shard_map/all_to_all | solution.py:143
  87.9 2.9 bitcast_convert_fusion
  90.7 2.8 gather_fusion.1
  93.5 1.0 copy.107
  94.5 2.9 fusion.26
  97.5 1.9 convolution_convert_fusion.1
  99.4 0.0 all-reduce.2.cloned.1.call-update
  99.4 0.0 all-gather.2.cloned.1.call-start
  99.5 0.0 copy-start.5
  99.5 3.2 convert_element_type.100
  102.6 43.5 %all-reduce.2.cloned.1.call-done = bf16[256,2560]{1,0:T(8,128)(2,1)} async-done(((bf16[256,2560]{1,0:T(8,128)(2,1)}), bf16[256,2560]{1,0:T(8,128)(2,1)}) %all-reduce.2.cloned.1.call-update) | async-done | bytes 1310736 | tf_op jit(solution)/shard_map/psum | solution.py:163
  146.2 1.1 fusion.34
  147.3 1.5 multiply_reduce_fusion.1
  148.9 2.1 multiply_convert_fusion.1
  151.0 0.0 all-gather.2.cloned.1.call-update
  151.0 0.0 reduce-scatter.2.cloned.1.call-start
  151.1 58.1 %all-gather.2.cloned.1.call-done = bf16[2048,2560]{1,0:T(8,128)(2,1)} async-done(((bf16[64,2560]{1,0:T(8,128)(2,1)}), bf16[2048,2560]{1,0:T(8,128)(2,1)}) %all-gather.2.cloned.1.call-update) | async-done | bytes 10485776 | tf_op jit(solution)/shard_map/all_gather | solution.py:168
  209.1 9.5 %fusion.68 = f32[2048,320]{0,1:T(8,128)} fusion(bf16[2048,2560]{1,0:T(8,128)(2,1)} %all-gather.2.cloned.1.call-done, bf16[2560,320]{0,1:T(8,128)(2,1)} %param.29), kind=kOutput, calls=%fused_computation.110 | convolution fusion | flops 3355443200 | bytes 14745600 | tf_op jit(solution)/shard_map/dot_general | solution.py:169
  218.7 15.6 %convolution_convert_fusion = bf16[2048,2560]{1,0:T(8,128)(2,1)} fusion(bf16[320,2560]{1,0:T(8,128)(2,1)} %param.31, bf16[2048,2560]{1,0:T(8,128)(2,1)} %all-gather.2.cloned.1.call-done, bf16[2560,320]{0,1:T(8,128)(2,1)} %param.30, f32[2048,320]{0,1:T(8,128)} %fusion.68), kind=kOutput, calls=%fused_computation.2 | convolution fusion | flops 6722682880 | bytes 26869760 | tf_op jit(solution)/shard_map/dot_general | solution.py:173
  234.3 0.0 reduce-scatter.2.cloned.1.call-update
  234.3 97.7 %reduce-scatter.2.cloned.1.call-done = bf16[64,2560]{1,0:T(8,128)(2,1)} async-done(((bf16[2048,2560]{1,0:T(8,128)(2,1)}), bf16[64,2560]{1,0:T(8,128)(2,1)}) %reduce-scatter.2.cloned.1.call-update) | async-done | bytes 327696 | tf_op jit(solution)/shard_map/reduce_scatter | solution.py:172
  332.0 1.1 fusion.35
  333.1 2.3 fusion.38
  (29 shorter events, 0.2 us)
Async XLA Ops:
  6.5 90.9 %copy-start = (bf16[512,2560]{1,0:T(8,128)(2,1)S(1)}, bf16[512,2560]{1,0:T(8,128)(2,1)}, u32[]{:S(2)}) copy-start(bf16[512,2560]{1,0:T(8,128)(2,1)} %param.26) | copy-start | bytes 7864324
  16.2 10.3 %copy-start.7 = (s32[256]{0:T(256)S(1)}, s32[256]{0:T(256)}, u32[]{:S(2)}) copy-start(s32[256]{0:T(256)} %param.35) | copy-start | bytes 3076
  16.2 10.4 %copy-start.9 = (f32[2560]{0:T(1024)S(1)}, f32[2560]{0:T(1024)}, u32[]{:S(2)}) copy-start(f32[2560]{0:T(1024)} %param.20) | copy-start | bytes 30724
  18.9 24.8 %all-to-all-start = ((bf16[32,32,512]{2,1,0:T(8,128)(2,1)}), bf16[32,32,512]{2,1,0:T(8,128)(2,1)}, u32[]{:S(2)}, u32[]{:S(2)}) async-start(bf16[32,32,512]{2,1,0:T(8,128)(2,1)} %bitcast.130), calls=%async_computation | async-start | bytes 2097152 | tf_op jit(solution)/shard_map/all_to_all | solution.py:138
  26.6 19.2 %copy-start.3 = (bf16[1,512,256]{2,1,0:T(8,128)(2,1)S(1)}, bf16[1,512,256]{2,1,0:T(8,128)(2,1)}, u32[]{:S(2)}) copy-start(bf16[1,512,256]{2,1,0:T(8,128)(2,1)} %param.33) | copy-start | bytes 786436
  47.9 1.9 copy-start.1
  47.9 7.1 %copy-start.8 = (bf16[1,512,256]{2,1,0:T(8,128)(2,1)S(1)}, bf16[1,512,256]{2,1,0:T(8,128)(2,1)}, u32[]{:S(2)}) copy-start(bf16[1,512,256]{2,1,0:T(8,128)(2,1)} %param.34) | copy-start | bytes 786436
  51.2 12.0 %all-to-all-start.1 = ((bf16[32,32,2]{1,2,0:T(2,128)(2,1)}), bf16[32,32,2]{1,2,0:T(2,128)(2,1)S(1)}, u32[]{:S(2)}, u32[]{:S(2)}) async-start(bf16[32,32,2]{1,2,0:T(2,128)(2,1)} %copy.99), calls=%async_computation.1 | async-start | bytes 32768 | tf_op jit(solution)/shard_map/all_to_all | solution.py:146
  60.6 10.3 %copy-start.11 = (f32[256]{0:T(256)S(1)}, f32[256]{0:T(256)}, u32[]{:S(2)}) copy-start(f32[256]{0:T(256)} %param.25) | copy-start | bytes 3076
  60.6 10.3 %copy-start.12 = (f32[256,256]{0,1:T(8,128)S(1)}, f32[256,256]{0,1:T(8,128)}, u32[]{:S(2)}) copy-start(f32[256,256]{0,1:T(8,128)} %get-tuple-element.12) | copy-start | bytes 786436
  63.2 24.7 %all-to-all-start.2 = ((bf16[32,32,512]{2,1,0:T(8,128)(2,1)}), bf16[32,32,512]{2,1,0:T(8,128)(2,1)}, u32[]{:S(2)}, u32[]{:S(2)}) async-start(bf16[32,32,512]{2,1,0:T(8,128)(2,1)} %convert_element_type.114), calls=%async_computation.2 | async-start | bytes 2097152 | tf_op jit(solution)/shard_map/all_to_all | solution.py:143
  70.7 75.5 %all-reduce.2.cloned.1.call-start = ((), (), s32[]{:S(2)}) async-start(), calls=%async_computation.4 | async-start | bytes 2621440 | tf_op jit(solution)/shard_map/psum | solution.py:163
  71.3 0.8 copy-start.2
  90.7 3.8 %copy-start.10 = (f32[2560]{0:T(1024)S(1)}, f32[2560]{0:T(1024)}, u32[]{:S(2)}) copy-start(f32[2560]{0:T(1024)} %param.20) | copy-start | bytes 30724
  99.4 47.9 %copy-start.4 = (f32[2560]{0:T(1024)S(1)}, f32[2560]{0:T(1024)}, u32[]{:S(2)}) copy-start(f32[2560]{0:T(1024)} %param.27) | copy-start | bytes 30724
  99.4 109.7 %all-gather.2.cloned.1.call-start = ((), (), s32[]{:S(2)}) async-start(), calls=%async_computation.5 | async-start | bytes 10813440 | tf_op jit(solution)/shard_map/all_gather | solution.py:168
  99.5 49.4 %copy-start.5 = (f32[2560]{0:T(1024)S(1)}, f32[2560]{0:T(1024)}, u32[]{:S(2)}) copy-start(f32[2560]{0:T(1024)} %param.28) | copy-start | bytes 30724
  151.0 181.0 %reduce-scatter.2.cloned.1.call-start = ((), (), s32[]{:S(2)}) async-start(), calls=%async_computation.6 | async-start | bytes 10813440 | tf_op jit(solution)/shard_map/reduce_scatter | solution.py:172
  234.3 98.9 %copy-start.6 = (f32[2560]{0:T(1024)S(1)}, f32[2560]{0:T(1024)}, u32[]{:S(2)}) copy-start(f32[2560]{0:T(1024)} %param.32) | copy-start | bytes 30724
Sparse Core Ops, SparseCore 0:
  99.5 46.5 all-reduce.1
  151.1 57.9 all-gather.1
  234.4 97.5 reduce-scatter.1
where the time goes:
time: 343 us; the launch traced here: 342 us
  waiting for transfers between devices  228 us (66%)
  matrix products  44.8 us (13%)
  other arithmetic  19.4 us (6%)
  starting transfers between devices  19.1 us (6%)
  local copies, waits for them, and re-layouts  17.5 us (5%)
  between operations  13.4 us (4%)
    reduce_scatter x1, waiting for transfers between devices, body(): lax.psum_scatter(jnp.dot(hidden, down_weight, preferred_element_type=jnp....  97.7 us
    all_gather x1, waiting for transfers between devices, body(): piece = lax.all_gather(ffw_in, 'req', axis=0, tiled=True)  58.1 us
    psum x1, waiting for transfers between devices, body(): lax.psum(partial_value.astype(jnp.bfloat16), 'mlp').astype(jnp.float32)  43.5 us
    dot_general x1, matrix products, body(): jnp.dot(hidden, down_weight, preferred_element_type=jnp.float32)  15.6 us
    all_to_all x1, waiting for transfers between devices, body(): lax.all_to_all(mixed.astype(jnp.bfloat16), 'req', split_axis=0, concat_ax...  14.6 us
    all_to_all x1, waiting for transfers between devices, body(): lax.all_to_all(outgoing, 'req', split_axis=0, concat_axis=0, tiled=True)  13.8 us
    dot_general x1, matrix products, body(): gate_proj = jnp.dot(piece, gate_weight, preferred_element_type=jnp.float32)  9.53 us
    all_to_all x1, starting transfers between devices, body(): lax.all_to_all(outgoing, 'req', split_axis=0, concat_axis=0, tiled=True)  7.56 us
  transfers between devices with their start and end apart: 6, of which 5 were waited for; matrix products, arithmetic and copies ran while one was open for 5% of the time, Pallas kernels for 0%

commit v1 on v0

--- a/solution.py
+++ b/solution.py
@@ -160,8 +160,9 @@
         .reshape(row_count, head_cols)
     )
     partial_value = jnp.dot(attended, out_weight, preferred_element_type=jnp.float32)
-    full_sum = lax.psum(partial_value.astype(jnp.bfloat16), "mlp").astype(jnp.float32)
-    summed = lax.dynamic_slice_in_dim(full_sum, mlp_index * quarter, quarter, 0)
+    summed = lax.psum_scatter(
+        partial_value.astype(jnp.bfloat16), "mlp", scatter_dimension=0, tiled=True
+    ).astype(jnp.float32)
     own_rows = lax.dynamic_slice_in_dim(states_f, mlp_index * quarter, quarter, 0)
     residual = own_rows + normed(summed, post_gain)
     ffw_in = normed(residual, ffw_gain).astype(jnp.bfloat16)

time: 343 us -> 319 us (0.930)
  waiting for transfers between devices: 228 us -> 204 us
    psum x1 -> x0, waiting for transfers between devices: 43.5 us -> none  [body(): lax.psum(partial_value.astype(jnp.bfloat16), 'mlp').astype(jnp.float32)]
    reduce_scatter x0 -> x1, waiting for transfers between devices: none -> 20.5 us  [body(): lax.psum_scatter(partial_value.astype(jnp.bfloat16), 'mlp', scatter_dimen...]
where the time goes in v1:
time: 319 us; the launch traced here: 318 us
  waiting for transfers between devices  204 us (64%)
  matrix products  44.8 us (14%)
  other arithmetic  19.3 us (6%)
  starting transfers between devices  19.1 us (6%)
  local copies, waits for them, and re-layouts  17.5 us (5%)
  between operations  13.4 us (4%)
    reduce_scatter x1, waiting for transfers between devices, body(): lax.psum_scatter(jnp.dot(hidden, down_weight, preferred_element_type=jnp....  97.7 us
    all_gather x1, waiting for transfers between devices, body(): piece = lax.all_gather(ffw_in, 'req', axis=0, tiled=True)  57.2 us
    reduce_scatter x1, waiting for transfers between devices, body(): lax.psum_scatter(partial_value.astype(jnp.bfloat16), 'mlp', scatter_dimen...  20.5 us
    dot_general x1, matrix products, body(): jnp.dot(hidden, down_weight, preferred_element_type=jnp.float32)  15.6 us
    all_to_all x1, waiting for transfers between devices, body(): lax.all_to_all(mixed.astype(jnp.bfloat16), 'req', split_axis=0, concat_ax...  14.6 us
    all_to_all x1, waiting for transfers between devices, body(): lax.all_to_all(outgoing, 'req', split_axis=0, concat_axis=0, tiled=True)  13.8 us
    dot_general x1, matrix products, body(): gate_proj = jnp.dot(piece, gate_weight, preferred_element_type=jnp.float32)  9.53 us
    all_to_all x1, starting transfers between devices, body(): lax.all_to_all(outgoing, 'req', split_axis=0, concat_axis=0, tiled=True)  7.56 us
  transfers between devices with their start and end apart: 6, of which 5 were waited for; matrix products, arithmetic and copies ran while one was open for 5% of the time, Pallas kernels for 0%

profile of v1, /device:TPU:0, one launch (start us, length us, event | category | flops | bytes accessed | tf_op | source)
XLA Modules:
  0.0 318.0 jit_solution(8338432984509761977)
XLA Ops:
  6.5 0.0 copy-start
  6.5 0.9 select_reduce_fusion
  7.5 0.2 fusion.29
  7.7 1.7 multiply_reduce_fusion
  9.4 0.7 broadcast_bitcast_fusion
  10.0 4.0 %fusion.66 = (f32[256,512]{1,0:T(8,128)}, f32[256,512]{1,0:T(8,128)}) fusion(bf16[2560,512]{1,0:T(8,128)(2,1)} %param.21, f32[2560]{0:T(1024)} %param.20, f32[256]{0:T(256)S(1)} %add_rsqrt_fusion.2, bf16[256,2560]{1,0:T(8,128)(2,1)} %param.19), kind=kOutput, calls=%fused_computation.108 | convolution fusion | flops 673841152 | bytes 4992000 | tf_op jit(solution)/shard_map/dot_general | solution.py:96
  14.1 1.4 mul.265
  15.5 0.3 reduce_sum.93
  15.8 0.3 mul.266
  16.2 0.0 copy-start.8
  16.2 0.0 copy-start.10
  16.3 1.2 multiply_convert_fusion.2
  17.4 1.5 convolution_convert_fusion.2
  18.9 7.6 %all-to-all-start = ((bf16[32,32,512]{2,1,0:T(8,128)(2,1)}), bf16[32,32,512]{2,1,0:T(8,128)(2,1)}, u32[]{:S(2)}, u32[]{:S(2)}) async-start(bf16[32,32,512]{2,1,0:T(8,128)(2,1)} %bitcast.130), calls=%async_computation | async-start | bytes 2097152 | tf_op jit(solution)/shard_map/all_to_all | solution.py:138
  26.5 0.0 copy-done.8
  26.5 0.1 fusion.47
  26.6 0.0 copy-start.4
  26.6 3.2 %multiply_reduce_fusion.2 = (f32[256]{0:T(256)S(1)}, f32[256,256]{0,1:T(8,128)}) fusion(bf16[2560,256]{1,0:T(8,128)(2,1)} %param.22, f32[2560]{0:T(1024)S(1)} %copy-done.10, f32[256]{0:T(256)S(1)} %add_rsqrt_fusion.2, bf16[256,2560]{1,0:T(8,128)(2,1)} %param.19), kind=kOutput, calls=%fused_computation.71 | convolution fusion | flops 338296576 | bytes 2895872 | tf_op jit(solution)/shard_map/dot_general | solution.py:100
  29.9 13.8 %all-to-all-done = bf16[32,32,512]{2,1,0:T(8,128)(2,1)} async-done(((bf16[32,32,512]{2,1,0:T(8,128)(2,1)}), bf16[32,32,512]{2,1,0:T(8,128)(2,1)}, u32[]{:S(2)}, u32[]{:S(2)}) %all-to-all-start) | async-done | bytes 1048608 | tf_op jit(solution)/shard_map/all_to_all | solution.py:138
  43.7 2.2 reshape.279
  45.9 2.0 bitcast_reduce_fusion
  47.9 0.0 copy-start.9
  47.9 1.9 copy-done.1
  49.8 0.7 fusion.1
  50.5 0.1 convert_element_type.106
  50.6 0.6 copy.99
  51.2 3.8 %all-to-all-start.1 = ((bf16[32,32,2]{1,2,0:T(2,128)(2,1)}), bf16[32,32,2]{1,2,0:T(2,128)(2,1)S(1)}, u32[]{:S(2)}, u32[]{:S(2)}) async-start(bf16[32,32,2]{1,2,0:T(2,128)(2,1)} %copy.99), calls=%async_computation.1 | async-start | bytes 32768 | tf_op jit(solution)/shard_map/all_to_all | solution.py:146
  55.0 3.5 %fusion.16 = bf16[1024,1,2,256]{3,0,2,1:T(8,128)(2,1)S(1)} fusion(f32[1024,2]{0,1:T(2,128)S(1)} %fusion.1, f32[1024,2]{0,1:T(2,128)S(1)} %get-tuple-element.9, f32[1024,2,512]{0,2,1:T(8,128)} %copy-done.1, bf16[1,512,256]{2,1,0:T(8,128)(2,1)S(1)} %copy-done.9), kind=kOutput, calls=%fused_computation.26 | convolution fusion | flops 541589504 | bytes 5521408 | tf_op jit(solution)/shard_map/rgqk,kgd->rgqd/dot_general | solution.py:54
  58.5 2.1 copy.106
  60.6 2.6 convert_element_type.114
  63.2 0.0 all-to-all-done.1
  63.2 7.5 %all-to-all-start.2 = ((bf16[32,32,512]{2,1,0:T(8,128)(2,1)}), bf16[32,32,512]{2,1,0:T(8,128)(2,1)}, u32[]{:S(2)}, u32[]{:S(2)}) async-start(bf16[32,32,512]{2,1,0:T(8,128)(2,1)} %convert_element_type.114), calls=%async_computation.2 | async-start | bytes 2097152 | tf_op jit(solution)/shard_map/all_to_all | solution.py:143
  70.7 0.2 reduce-scatter.3.cloned.1.call-start
  70.9 0.4 fusion.67
  71.3 0.1 fusion.40
  71.4 0.7 copy-done.3
  72.1 0.3 copy.114
  72.4 0.7 gather_fusion
  73.1 0.1 copy.102
  73.2 14.6 %all-to-all-done.2 = bf16[32,32,512]{2,1,0:T(8,128)(2,1)} async-done(((bf16[32,32,512]{2,1,0:T(8,128)(2,1)}), bf16[32,32,512]{2,1,0:T(8,128)(2,1)}, u32[]{:S(2)}, u32[]{:S(2)}) %all-to-all-start.2) | async-done | bytes 1048608 | tf_op jit(solution)/shard_map/all_to_all | solution.py:143
  87.9 2.9 bitcast_convert_fusion
  90.7 2.8 gather_fusion.1
  93.5 1.0 copy.107
  94.5 2.9 fusion.26
  97.4 0.0 copy-done
  97.5 1.9 convolution_convert_fusion.1
  99.4 0.0 reduce-scatter.3.cloned.1.call-update
  99.4 0.0 all-gather.2.cloned.1.call-start
  99.5 0.0 copy-start.6
  99.5 3.2 convert_element_type.100
  102.6 20.5 %reduce-scatter.3.cloned.1.call-done = bf16[64,2560]{1,0:T(8,128)(2,1)} async-done(((bf16[256,2560]{1,0:T(8,128)(2,1)}), bf16[64,2560]{1,0:T(8,128)(2,1)}) %reduce-scatter.3.cloned.1.call-update) | async-done | bytes 327696 | tf_op jit(solution)/shard_map/reduce_scatter | solution.py:163
  123.2 1.1 fusion.32
  124.3 1.5 multiply_reduce_fusion.1
  125.8 0.0 copy-done.6
  125.9 2.1 multiply_convert_fusion.1
  128.0 0.0 all-gather.2.cloned.1.call-update
  128.0 0.0 reduce-scatter.5.cloned.1.call-start
  128.1 57.2 %all-gather.2.cloned.1.call-done = bf16[2048,2560]{1,0:T(8,128)(2,1)} async-done(((bf16[64,2560]{1,0:T(8,128)(2,1)}), bf16[2048,2560]{1,0:T(8,128)(2,1)}) %all-gather.2.cloned.1.call-update) | async-done | bytes 10485776 | tf_op jit(solution)/shard_map/all_gather | solution.py:169
  185.3 9.5 %fusion.68 = f32[2048,320]{0,1:T(8,128)} fusion(bf16[2048,2560]{1,0:T(8,128)(2,1)} %all-gather.2.cloned.1.call-done, bf16[2560,320]{0,1:T(8,128)(2,1)} %param.29), kind=kOutput, calls=%fused_computation.110 | convolution fusion | flops 3355443200 | bytes 14745600 | tf_op jit(solution)/shard_map/dot_general | solution.py:170
  194.8 15.6 %convolution_convert_fusion = bf16[2048,2560]{1,0:T(8,128)(2,1)} fusion(bf16[320,2560]{1,0:T(8,128)(2,1)} %param.31, bf16[2048,2560]{1,0:T(8,128)(2,1)} %all-gather.2.cloned.1.call-done, bf16[2560,320]{0,1:T(8,128)(2,1)} %param.30, f32[2048,320]{0,1:T(8,128)} %fusion.68), kind=kOutput, calls=%fused_computation.2 | convolution fusion | flops 6722682880 | bytes 26869760 | tf_op jit(solution)/shard_map/dot_general | solution.py:174
  210.4 0.0 reduce-scatter.5.cloned.1.call-update
  210.4 97.7 %reduce-scatter.5.cloned.1.call-done = bf16[64,2560]{1,0:T(8,128)(2,1)} async-done(((bf16[2048,2560]{1,0:T(8,128)(2,1)}), bf16[64,2560]{1,0:T(8,128)(2,1)}) %reduce-scatter.5.cloned.1.call-update) | async-done | bytes 327696 | tf_op jit(solution)/shard_map/reduce_scatter | solution.py:173
  308.1 1.1 fusion.35
  309.3 2.2 fusion.38
  (31 shorter events, 0.2 us)
Async XLA Ops:
  6.5 90.9 %copy-start = (bf16[512,2560]{1,0:T(8,128)(2,1)S(1)}, bf16[512,2560]{1,0:T(8,128)(2,1)}, u32[]{:S(2)}) copy-start(bf16[512,2560]{1,0:T(8,128)(2,1)} %param.26) | copy-start | bytes 7864324
  16.2 10.3 %copy-start.8 = (s32[256]{0:T(256)S(1)}, s32[256]{0:T(256)}, u32[]{:S(2)}) copy-start(s32[256]{0:T(256)} %param.35) | copy-start | bytes 3076
  16.2 10.4 %copy-start.10 = (f32[2560]{0:T(1024)S(1)}, f32[2560]{0:T(1024)}, u32[]{:S(2)}) copy-start(f32[2560]{0:T(1024)} %param.20) | copy-start | bytes 30724
  18.9 24.8 %all-to-all-start = ((bf16[32,32,512]{2,1,0:T(8,128)(2,1)}), bf16[32,32,512]{2,1,0:T(8,128)(2,1)}, u32[]{:S(2)}, u32[]{:S(2)}) async-start(bf16[32,32,512]{2,1,0:T(8,128)(2,1)} %bitcast.130), calls=%async_computation | async-start | bytes 2097152 | tf_op jit(solution)/shard_map/all_to_all | solution.py:138
  26.6 19.2 %copy-start.4 = (bf16[1,512,256]{2,1,0:T(8,128)(2,1)S(1)}, bf16[1,512,256]{2,1,0:T(8,128)(2,1)}, u32[]{:S(2)}) copy-start(bf16[1,512,256]{2,1,0:T(8,128)(2,1)} %param.33) | copy-start | bytes 786436
  47.9 1.9 copy-start.1
  47.9 7.1 %copy-start.9 = (bf16[1,512,256]{2,1,0:T(8,128)(2,1)S(1)}, bf16[1,512,256]{2,1,0:T(8,128)(2,1)}, u32[]{:S(2)}) copy-start(bf16[1,512,256]{2,1,0:T(8,128)(2,1)} %param.34) | copy-start | bytes 786436
  51.2 12.0 %all-to-all-start.1 = ((bf16[32,32,2]{1,2,0:T(2,128)(2,1)}), bf16[32,32,2]{1,2,0:T(2,128)(2,1)S(1)}, u32[]{:S(2)}, u32[]{:S(2)}) async-start(bf16[32,32,2]{1,2,0:T(2,128)(2,1)} %copy.99), calls=%async_computation.1 | async-start | bytes 32768 | tf_op jit(solution)/shard_map/all_to_all | solution.py:146
  60.6 10.3 %copy-start.12 = (f32[256]{0:T(256)S(1)}, f32[256]{0:T(256)}, u32[]{:S(2)}) copy-start(f32[256]{0:T(256)} %param.25) | copy-start | bytes 3076
  60.6 10.3 %copy-start.13 = (f32[256,256]{0,1:T(8,128)S(1)}, f32[256,256]{0,1:T(8,128)}, u32[]{:S(2)}) copy-start(f32[256,256]{0,1:T(8,128)} %get-tuple-element.12) | copy-start | bytes 786436
  63.2 24.7 %all-to-all-start.2 = ((bf16[32,32,512]{2,1,0:T(8,128)(2,1)}), bf16[32,32,512]{2,1,0:T(8,128)(2,1)}, u32[]{:S(2)}, u32[]{:S(2)}) async-start(bf16[32,32,512]{2,1,0:T(8,128)(2,1)} %convert_element_type.114), calls=%async_computation.2 | async-start | bytes 2097152 | tf_op jit(solution)/shard_map/all_to_all | solution.py:143
  70.7 52.5 %reduce-scatter.3.cloned.1.call-start = ((), (), s32[]{:S(2)}) async-start(), calls=%async_computation.5 | async-start | bytes 1638400 | tf_op jit(solution)/shard_map/reduce_scatter | solution.py:163
  71.3 0.8 copy-start.3
  90.7 3.8 %copy-start.11 = (f32[2560]{0:T(1024)S(1)}, f32[2560]{0:T(1024)}, u32[]{:S(2)}) copy-start(f32[2560]{0:T(1024)} %param.20) | copy-start | bytes 30724
  99.4 24.9 %copy-start.5 = (f32[2560]{0:T(1024)S(1)}, f32[2560]{0:T(1024)}, u32[]{:S(2)}) copy-start(f32[2560]{0:T(1024)} %param.27) | copy-start | bytes 30724
  99.4 85.8 %all-gather.2.cloned.1.call-start = ((), (), s32[]{:S(2)}) async-start(), calls=%async_computation.6 | async-start | bytes 10813440 | tf_op jit(solution)/shard_map/all_gather | solution.py:169
  99.5 26.4 %copy-start.6 = (f32[2560]{0:T(1024)S(1)}, f32[2560]{0:T(1024)}, u32[]{:S(2)}) copy-start(f32[2560]{0:T(1024)} %param.28) | copy-start | bytes 30724
  128.0 180.1 %reduce-scatter.5.cloned.1.call-start = ((), (), s32[]{:S(2)}) async-start(), calls=%async_computation.7 | async-start | bytes 10813440 | tf_op jit(solution)/shard_map/reduce_scatter | solution.py:173
  210.4 98.9 %copy-start.2 = (bf16[64,2560]{1,0:T(8,128)(2,1)S(1)}, bf16[64,2560]{1,0:T(8,128)(2,1)}, u32[]{:S(2)}) copy-start(bf16[64,2560]{1,0:T(8,128)(2,1)} %reduce-scatter.3.cloned.1.call-done) | copy-start | bytes 983044
  210.4 98.9 %copy-start.7 = (f32[2560]{0:T(1024)S(1)}, f32[2560]{0:T(1024)}, u32[]{:S(2)}) copy-start(f32[2560]{0:T(1024)} %param.32) | copy-start | bytes 30724
Sparse Core Ops, SparseCore 0:
  99.5 23.5 reduce-scatter.2
  128.1 57.0 all-gather.1
  210.6 97.5 reduce-scatter.4
